TPU v7x, 256 devices: a whole 4x4x8 slice. The times are simulated.
256 devices in a mesh: outer: 8 (over z), inner: 32 (over y, x, core).
Axes of the slice: x: 4, y: 4, z: 8, core: 2. Of those that a mesh axis runs over, the one named last changes fastest.
Arguments:
- context: bfloat16 [32768, 4096], P(('outer', 'inner')), may hold values from -5 to 5
- query_acts: bfloat16 [64, 4096], replicated, may hold values from -5 to 5
- norm_gain: float32 [4096], replicated, may hold values from 0.25 to 1.75
- w_query: bfloat16 [4096, 2048], P('inner'), may hold values from -0.078125 to 0.078125
- w_key: bfloat16 [4096, 512], P('inner'), may hold values from -0.453125 to 0.453125
- value_weight: bfloat16 [4096, 512], P('inner'), may hold values from -0.09375 to 0.09375
- lengths: int32 [256], replicated, may hold values from 64 to 128, as said below
Outputs:
- block_out: bfloat16 [32768, 2048], P(('outer', 'inner'))
- query_out: bfloat16 [64, 2048], replicated
Inputs may be any that keep to these rules, and one draw needn't show every extreme that they name: `lengths`: valid tokens of a block are its first ones; the rest of it is padding.
All inputs are finite; a program needn't handle non-finite values.
Results may differ from a plain program's by a relative error of at most 0.004.
The roundings to bfloat16 on the way count: a program that leaves them out, or rounds other values in their place, can miss the bound.
Values may be sent and summed in bfloat16 or wider, within the bound.
No kernel may reach another device: no remote copies, remote signals or barrier semaphores. Data moves between devices by JAX's collectives and lax.ppermute only.
A program may use at most 320 MiB of HBM per device.

v0:
```python
import jax
import jax.numpy as jnp
from jax import lax
from jax.sharding import PartitionSpec as P

QUERY_HEADS = 16
KEY_VALUE_HEADS = 4
HEAD_SIZE = 128
epsilon = 1e-05


def broadcast(block, axis, owner):
    block = jnp.where(lax.axis_index(axis) == owner, block, jnp.zeros_like(block))
    return lax.psum(block, axis)


def normalize(matrix, norm_gain):
    widened = matrix.astype(jnp.float32)
    factor = lax.rsqrt(jnp.mean(widened * widened, axis=-1, keepdims=True) + epsilon)
    return (widened * factor * norm_gain).astype(jnp.bfloat16)


def attend_part(query_rows, key_row_block, value_matrix, allowed):
    count_of_rows = query_rows.shape[0]
    head_groups = query_rows.reshape(
        count_of_rows, KEY_VALUE_HEADS, QUERY_HEADS // KEY_VALUE_HEADS, HEAD_SIZE
    )
    per_head_keys = key_row_block.reshape(key_row_block.shape[0], KEY_VALUE_HEADS, HEAD_SIZE)
    per_head_values = value_matrix.reshape(value_matrix.shape[0], KEY_VALUE_HEADS, HEAD_SIZE)
    scores = jnp.einsum(
        "rhgd,khd->hgrk", head_groups, per_head_keys, preferred_element_type=jnp.float32
    ) * HEAD_SIZE ** (-0.5)
    scores = jnp.where(allowed, scores, -jnp.inf)
    maxima = jnp.max(scores, axis=-1)
    weights = jnp.exp(scores - maxima[..., None])
    sum_exp = jnp.sum(weights, axis=-1)
    numerator = jnp.einsum(
        "hgrk,khd->rhgd",
        weights.astype(jnp.bfloat16),
        per_head_values,
        preferred_element_type=jnp.float32,
    )
    return (
        maxima.reshape(QUERY_HEADS, count_of_rows),
        sum_exp.reshape(QUERY_HEADS, count_of_rows),
        numerator.reshape(count_of_rows, QUERY_HEADS * HEAD_SIZE),
    )


def spread(factor):
    return jnp.repeat(factor.T, HEAD_SIZE, axis=1)


def combine(former, latter):
    maxima = jnp.maximum(former[0], latter[0])
    scale_one = jnp.exp(former[0] - maxima)
    scale_two = jnp.exp(latter[0] - maxima)
    return (
        maxima,
        former[1] * scale_one + latter[1] * scale_two,
        former[2] * spread(scale_one) + latter[2] * spread(scale_two),
    )


def finish(pieces):
    return (pieces[2] / spread(pieces[1])).astype(jnp.bfloat16)


def share_anchor(stacked):
    return broadcast(stacked, ("outer", "inner"), 0)


def per_device(context, query_acts, norm_gain, w_query, w_key, value_weight, lengths):
    block_rows = context.shape[0]
    normed = jnp.concatenate(
        [normalize(context, norm_gain), normalize(query_acts, norm_gain)], axis=0
    )

    def apply_weight(whole_weight):
        return jnp.dot(normed, whole_weight, preferred_element_type=jnp.float32).astype(
            jnp.bfloat16
        )

    whole_q, whole_k, whole_v = (
        lax.all_gather(w_query, "inner", axis=0, tiled=True),
        lax.all_gather(w_key, "inner", axis=0, tiled=True),
        lax.all_gather(value_weight, "inner", axis=0, tiled=True),
    )
    projected_k = apply_weight(whole_k)
    projected_v = apply_weight(whole_v)
    anchor = share_anchor(jnp.stack([projected_k[:block_rows], projected_v[:block_rows]]))
    projected_q = apply_weight(whole_q)
    position = lax.axis_index(("outer", "inner"))
    own_length = lengths[position]
    anchor_length = lengths[0]
    places = jnp.arange(block_rows, dtype=jnp.int32)
    causal = places[:, None] >= places[None, :]
    block_q = projected_q[:block_rows]
    block_k = projected_k[:block_rows]
    block_v = projected_v[:block_rows]
    query_q = projected_q[block_rows:]
    query_k = projected_k[block_rows:]
    query_v = projected_v[block_rows:]
    query_count = query_q.shape[0]
    own_allowed = causal & (places[None, :] < own_length)
    anchor_allowed = jnp.broadcast_to(
        (places[None, :] < anchor_length) & (position > 0), (block_rows, block_rows)
    )
    allowed = jnp.concatenate([anchor_allowed, own_allowed], axis=1)
    key_row_block = jnp.concatenate([anchor[0], block_k], axis=0)
    value_rows = jnp.concatenate([anchor[1], block_v], axis=0)
    block_out = finish(attend_part(block_q, key_row_block, value_rows, allowed))
    reached = jnp.broadcast_to(places[None, :] < own_length, (query_count, block_rows))
    block_part = attend_part(query_q, block_k, block_v, reached)
    highest = lax.pmax(block_part[0], ("outer", "inner"))
    rescale = jnp.exp(block_part[0] - highest)
    summed_parts = lax.psum(
        (block_part[1] * rescale, block_part[2] * spread(rescale)), ("outer", "inner")
    )
    merged = (highest, summed_parts[0], summed_parts[1])
    query_places = jnp.arange(query_count, dtype=jnp.int32)
    self_part = attend_part(
        query_q, query_k, query_v, query_places[:, None] >= query_places[None, :]
    )
    return (block_out, finish(combine(merged, self_part)))


def solution(mesh):
    in_specs = (
        P(("outer", "inner"), None),
        P(),
        P(),
        P("inner", None),
        P("inner", None),
        P("inner", None),
        P(),
    )
    out_specs = (P(("outer", "inner"), None), P())
    return jax.shard_map(
        per_device, mesh=mesh, in_specs=in_specs, out_specs=out_specs, check_vma=False
    )
```

profile of v0, /device:TPU:2, one launch (start us, length us, event | category | flops | bytes accessed | tf_op | source)
XLA Modules:
  0.0 875.9 jit_solution(4082930749184454192)
XLA Ops:
  7.2 0.7 all-gather.4.cloned.1.call-update
  8.0 0.7 all-gather.6.cloned.1.call-update
  8.7 1.2 fusion.9
  10.0 1.5 fusion
  11.5 0.9 fusion.11
  12.5 0.3 fusion.2
  12.8 51.5 %all-gather.4.cloned.1.call-done = bf16[4096,512]{1,0:T(8,128)(2,1)} async-done(((bf16[128,512]{1,0:T(8,128)(2,1)}), bf16[4096,512]{1,0:T(8,128)(2,1)}) %all-gather.4.cloned.1.call-update) | async-done | bytes 4194320 | tf_op jit(solution)/shard_map/all_gather | solution.py:86
  64.3 3.2 convolution_convert_fusion.2
  67.6 49.9 %all-gather.6.cloned.1.call-done = bf16[4096,512]{1,0:T(8,128)(2,1)} async-done(((bf16[128,512]{1,0:T(8,128)(2,1)}), bf16[4096,512]{1,0:T(8,128)(2,1)}) %all-gather.6.cloned.1.call-update) | async-done | bytes 4194320 | tf_op jit(solution)/shard_map/all_gather | solution.py:87
  117.5 3.2 convolution_convert_fusion.1
  120.7 0.7 maximum_select_fusion
  121.5 0.5 all-gather.8.cloned.1.call-update
  122.1 0.6 fusion.52
  122.7 0.6 compare_and_fusion
  123.2 0.6 iota_compare_fusion.2
  124.1 0.8 copy.28
  124.9 0.7 concatenate.28
  125.6 0.6 reshape.106
  126.2 0.6 reshape.109
  126.9 246.7 %all-reduce.3.cloned.1.call-done = bf16[2,128,512]{2,1,0:T(8,128)(2,1)} async-done(((bf16[2,128,512]{2,1,0:T(8,128)(2,1)}), bf16[2,128,512]{2,1,0:T(8,128)(2,1)}) %all-reduce.3.cloned.1.call-update) | async-done | bytes 262160 | tf_op jit(solution)/shard_map/psum | solution.py:14
  373.5 1.0 fusion.49
  374.6 0.8 copy.56
  375.4 76.8 %all-gather.8.cloned.1.call-done = bf16[4096,2048]{1,0:T(8,128)(2,1)} async-done(((bf16[128,2048]{1,0:T(8,128)(2,1)}), bf16[4096,2048]{1,0:T(8,128)(2,1)}) %all-gather.8.cloned.1.call-update) | async-done | bytes 16777232 | tf_op jit(solution)/shard_map/all_gather | solution.py:85
  452.2 7.7 convolution_convert_fusion
  459.9 0.4 reshape.98
  460.3 0.5 fusion.53
  460.8 0.3 fusion.3
  461.2 0.5 fusion.12
  461.8 0.3 copy.34
  462.4 0.3 copy-done.9
  462.7 0.4 fusion.54
  463.1 76.0 %pmax.7 = f32[16,64]{1,0:T(8,128)S(1)} all-reduce(f32[16,64]{1,0:T(8,128)S(1)} %bitcast.97), channel_id=1, replica_groups=mesh['outer'=8,'inner'=32] {'outer','inner'}, use_global_device_ids=true, to_apply=%region_6.7 | all-reduce | flops 1024 | bytes 8192 | tf_op jit(solution)/shard_map/pmax | solution.py:115
  539.1 0.4 fusion.19
  539.5 74.4 %psum.23 = f32[16,64]{1,0:T(8,128)S(1)} all-reduce(f32[16,64]{1,0:T(8,128)S(1)} %get-tuple-element.13), channel_id=1, replica_groups=mesh['outer'=8,'inner'=32] {'outer','inner'}, use_global_device_ids=true, to_apply=%region_10.11 | all-reduce | flops 1024 | bytes 8192 | tf_op jit(solution)/shard_map/psum | solution.py:117
  614.0 0.4 fusion.55
  614.6 0.3 convolution_bitcast_fusion
  614.9 0.3 copy.45
  615.2 0.2 reshape.110
  615.5 0.3 convolution_bitcast_fusion.1
  615.8 0.3 copy.38
  616.2 0.2 reshape.103
  616.7 1.0 bitcast_multiply_fusion.2
  617.8 0.3 broadcast_in_dim.68
  618.2 1.2 fusion.14
  619.3 247.2 %all-reduce.5.cloned.1.call-done = f32[64,2048]{1,0:T(8,128)} async-done(((f32[64,2048]{1,0:T(8,128)}), f32[64,2048]{1,0:T(8,128)}) %all-reduce.5.cloned.1.call-update) | async-done | bytes 524304 | tf_op jit(solution)/shard_map/psum | solution.py:117
  866.7 0.2 broadcast_in_dim.75
  866.9 0.2 broadcast_in_dim.74
  867.1 2.2 fusion.16
  (58 shorter events, 2.0 us)
Async XLA Ops:
  7.2 4.4 copy-start.1
  7.2 5.3 copy-start
  7.2 5.3 copy-start.10
  7.2 57.1 %all-gather.4.cloned.1.call-start = ((), (), s32[]{:S(2)}) async-start(), calls=%async_computation | async-start | bytes 4325376 | tf_op jit(solution)/shard_map/all_gather | solution.py:86
  7.9 109.5 %all-gather.6.cloned.1.call-start = ((), (), s32[]{:S(2)}) async-start(), calls=%async_computation.1 | async-start | bytes 4325376 | tf_op jit(solution)/shard_map/all_gather | solution.py:87
  8.7 364.9 %all-reduce.3.cloned.1.call-start = ((), (), s32[]{:S(2)}) async-start(), calls=%async_computation.2 | async-start | bytes 524288 | tf_op jit(solution)/shard_map/psum | solution.py:14
  12.5 105.0 %copy-start.3 = (bf16[64,4096]{1,0:T(8,128)(2,1)}, bf16[64,4096]{1,0:T(8,128)(2,1)S(1)}, u32[]{:S(2)}) copy-start(bf16[64,4096]{1,0:T(8,128)(2,1)S(1)} %fusion.11) | copy-start | bytes 1572868
  67.6 54.5 %copy-start.11 = (s32[256]{0:T(256)S(1)}, s32[256]{0:T(256)}, u32[]{:S(2)}) copy-start(s32[256]{0:T(256)} %param.13) | copy-start | bytes 3076
  120.6 331.5 %copy-start.4 = (bf16[64,4096]{1,0:T(8,128)(2,1)S(1)}, bf16[64,4096]{1,0:T(8,128)(2,1)}, u32[]{:S(2)}) copy-start(bf16[64,4096]{1,0:T(8,128)(2,1)} %copy-done.3) | copy-start | bytes 1572868
  121.4 330.7 %all-gather.8.cloned.1.call-start = ((), (), s32[]{:S(2)}) async-start(), calls=%async_computation.3 | async-start | bytes 17301504 | tf_op jit(solution)/shard_map/all_gather | solution.py:85
  122.0 744.5 %all-reduce.5.cloned.1.call-start = ((), (), s32[]{:S(2)}) async-start(), calls=%async_computation.4 | async-start | bytes 1048576 | tf_op jit(solution)/shard_map/psum | solution.py:117
  459.8 0.9 copy-start.2
  460.3 0.9 copy-start.5
  460.3 1.0 copy-start.6
  461.2 1.0 slice-start
  461.7 0.9 copy-start.9
  461.8 152.2 %copy-start.8 = (bf16[64,4,128]{2,1,0:T(4,128)(2,1)S(1)}, bf16[64,4,128]{2,1,0:T(4,128)(2,1)}, u32[]{:S(2)}) copy-start(bf16[64,4,128]{2,1,0:T(4,128)(2,1)} %reshape.106) | copy-start | bytes 196612
  462.1 152.5 %copy-start.7 = (bf16[64,4,128]{2,1,0:T(4,128)(2,1)S(1)}, bf16[64,4,128]{2,1,0:T(4,128)(2,1)}, u32[]{:S(2)}) copy-start(bf16[64,4,128]{2,1,0:T(4,128)(2,1)} %reshape.109) | copy-start | bytes 196612
Sparse Core Ops, SparseCore 0:
  10.6 53.7 all-gather.3
  66.9 50.5 all-gather.5
  123.5 250.0 all-reduce.2
  375.9 76.1 all-gather.7
  617.9 248.6 all-reduce.4
where the time goes:
time: 876 us
  waiting for transfers between devices  674 us (77%)
  blocking collectives  150 us (17%)
  matrix products  16.3 us (2%)
  between operations  14.2 us (2%)
  other arithmetic  11.4 us (1%)
  local copies, waits for them, and re-layouts  9.33 us (1%)
    psum x1, waiting for transfers between devices, per_device(): lax.psum((block_part[1] * rescale, block_part[2] * spread(rescale)), ('ou...  247 us
    psum x1, waiting for transfers between devices, broadcast(): return lax.psum(block, axis)  247 us
    all_gather x1, waiting for transfers between devices, per_device(): lax.all_gather(w_query, 'inner', axis=0, tiled=True)  76.8 us
    pmax x1, blocking collectives, per_device(): highest = lax.pmax(block_part[0], ('outer', 'inner'))  76 us
    psum x1, blocking collectives, per_device(): lax.psum((block_part[1] * rescale, block_part[2] * spread(rescale)), ('ou...  74.4 us
    all_gather x1, waiting for transfers between devices, per_device(): lax.all_gather(w_key, 'inner', axis=0, tiled=True)  51.5 us
    all_gather x1, waiting for transfers between devices, per_device(): lax.all_gather(value_weight, 'inner', axis=0, tiled=True)  49.9 us
  transfers between devices with their start and end apart: 5, of which 5 were waited for; matrix products, arithmetic and copies ran while one was open for 2% of the time, Pallas kernels for 0%

commit v1 on v0

--- a/solution.py
+++ b/solution.py
@@ -114,9 +114,8 @@
     block_part = attend_part(query_q, block_k, block_v, reached)
     highest = lax.pmax(block_part[0], ("outer", "inner"))
     rescale = jnp.exp(block_part[0] - highest)
-    summed_parts = lax.psum(
-        (block_part[1] * rescale, block_part[2] * spread(rescale)), ("outer", "inner")
-    )
+    one_axis = lax.psum((block_part[1] * rescale, block_part[2] * spread(rescale)), "inner")
+    summed_parts = lax.psum(one_axis, "outer")
     merged = (highest, summed_parts[0], summed_parts[1])
     query_places = jnp.arange(query_count, dtype=jnp.int32)
     self_part = attend_part(

time: 876 us -> 815 us (0.930)
  waiting for transfers between devices: 674 us -> 612 us
    psum x1 -> x2, waiting for transfers between devices: 247 us -> 182 us  [the longest x1 110 us: per_device(): lax.psum((block_part[1] * rescale, block_part[2] * spread(rescale)), 'inn...]
    psum x1 -> x2, blocking collectives: 74.4 us -> 76.7 us  [the longest x1 60.3 us: per_device(): lax.psum((block_part[1] * rescale, block_part[2] * spread(rescale)), 'inn...]
  transfers between devices with their start and end apart: 5 -> 6, of which waited for: 5 -> 6; matrix products, arithmetic and copies ran while one was open for 2% -> 2% of each run, Pallas kernels for 0% -> 0%
where the time goes in v1:
time: 815 us; the launch traced here: 814 us
  waiting for transfers between devices  612 us (75%)
  blocking collectives  153 us (19%)
  matrix products  17.1 us (2%)
  between operations  14.5 us (2%)
  other arithmetic  11.5 us (1%)
    psum x1, waiting for transfers between devices, broadcast(): return lax.psum(block, axis)  249 us
    psum x1, waiting for transfers between devices, per_device(): lax.psum((block_part[1] * rescale, block_part[2] * spread(rescale)), 'inn...  110 us
    all_gather x1, waiting for transfers between devices, per_device(): lax.all_gather(w_query, 'inner', axis=0, tiled=True)  77.4 us
    pmax x1, blocking collectives, per_device(): highest = lax.pmax(block_part[0], ('outer', 'inner'))  76 us
    psum x1, waiting for transfers between devices, per_device(): summed_parts = lax.psum(one_axis, 'outer')  72.1 us
    psum x1, blocking collectives, per_device(): lax.psum((block_part[1] * rescale, block_part[2] * spread(rescale)), 'inn...  60.3 us
    all_gather x1, waiting for transfers between devices, per_device(): lax.all_gather(w_key, 'inner', axis=0, tiled=True)  51.5 us
    all_gather x1, waiting for transfers between devices, per_device(): lax.all_gather(value_weight, 'inner', axis=0, tiled=True)  49.9 us
  transfers between devices with their start and end apart: 6, of which 6 were waited for; matrix products, arithmetic and copies ran while one was open for 2% of the time, Pallas kernels for 0%

profile of v1, /device:TPU:2, one launch (start us, length us, event | category | flops | bytes accessed | tf_op | source)
XLA Modules:
  0.0 814.2 jit_solution(17129923751523917955)
XLA Ops:
  7.2 0.7 all-gather.4.cloned.1.call-update
  8.0 0.7 all-gather.6.cloned.1.call-update
  8.7 1.2 fusion.9
  10.0 1.5 fusion
  11.5 0.9 fusion.11
  12.5 0.3 fusion.2
  12.8 51.5 %all-gather.4.cloned.1.call-done = bf16[4096,512]{1,0:T(8,128)(2,1)} async-done(((bf16[128,512]{1,0:T(8,128)(2,1)}), bf16[4096,512]{1,0:T(8,128)(2,1)}) %all-gather.4.cloned.1.call-update) | async-done | bytes 4194320 | tf_op jit(solution)/shard_map/all_gather | solution.py:86
  64.3 3.2 convolution_convert_fusion.2
  67.6 49.9 %all-gather.6.cloned.1.call-done = bf16[4096,512]{1,0:T(8,128)(2,1)} async-done(((bf16[128,512]{1,0:T(8,128)(2,1)}), bf16[4096,512]{1,0:T(8,128)(2,1)}) %all-gather.6.cloned.1.call-update) | async-done | bytes 4194320 | tf_op jit(solution)/shard_map/all_gather | solution.py:87
  117.5 3.2 convolution_convert_fusion.1
  120.6 0.7 maximum_select_fusion
  121.5 0.5 all-gather.8.cloned.1.call-update
  122.0 0.6 fusion.52
  122.7 0.7 compare_and_fusion
  123.3 0.6 iota_compare_fusion.2
  124.5 249.0 %all-reduce.4.cloned.1.call-done = bf16[2,128,512]{2,1,0:T(8,128)(2,1)} async-done(((bf16[2,128,512]{2,1,0:T(8,128)(2,1)}), bf16[2,128,512]{2,1,0:T(8,128)(2,1)}) %all-reduce.4.cloned.1.call-update) | async-done | bytes 262160 | tf_op jit(solution)/shard_map/psum | solution.py:14
  373.5 1.0 fusion.49
  374.7 77.4 %all-gather.8.cloned.1.call-done = bf16[4096,2048]{1,0:T(8,128)(2,1)} async-done(((bf16[128,2048]{1,0:T(8,128)(2,1)}), bf16[4096,2048]{1,0:T(8,128)(2,1)}) %all-gather.8.cloned.1.call-update) | async-done | bytes 16777232 | tf_op jit(solution)/shard_map/all_gather | solution.py:85
  452.2 7.7 convolution_convert_fusion
  459.9 0.4 reshape.98
  460.5 0.4 fusion.54
  460.9 76.0 %pmax.7 = f32[16,64]{1,0:T(8,128)S(1)} all-reduce(f32[16,64]{1,0:T(8,128)S(1)} %bitcast.97), channel_id=1, replica_groups=mesh['outer'=8,'inner'=32] {'outer','inner'}, use_global_device_ids=true, to_apply=%region_6.7 | all-reduce | flops 1024 | bytes 8192 | tf_op jit(solution)/shard_map/pmax | solution.py:115
  536.9 0.4 fusion.19
  537.3 60.3 %psum.38 = f32[16,64]{1,0:T(8,128)S(1)} all-reduce(f32[16,64]{1,0:T(8,128)S(1)} %get-tuple-element.13), channel_id=1, replica_groups=mesh['outer'=8,'inner'=32] {'inner'}, use_global_device_ids=true, to_apply=%region_11.12 | all-reduce | flops 1024 | bytes 8192 | tf_op jit(solution)/shard_map/psum | solution.py:117
  597.6 16.4 %psum.39 = f32[16,64]{1,0:T(8,128)S(1)} all-reduce(f32[16,64]{1,0:T(8,128)S(1)} %psum.38), channel_id=1, replica_groups=mesh['outer'=8,'inner'=32] {'outer'}, use_global_device_ids=true, to_apply=%region_12.13 | all-reduce | flops 1024 | bytes 8192 | tf_op jit(solution)/shard_map/psum | solution.py:118
  614.0 0.3 convolution_bitcast_fusion.1
  614.4 0.3 copy.38
  614.7 0.2 reshape.103
  615.0 0.2 broadcast_in_dim.71
  615.2 1.0 bitcast_multiply_fusion.2
  616.3 0.2 all-reduce.8.cloned.1.call-start
  616.5 0.4 fusion.55
  617.0 0.5 fusion.53
  617.5 0.5 fusion.12
  618.0 1.1 convolution_bitcast_fusion
  619.1 109.7 %all-reduce.6.cloned.1.call-done = f32[64,2048]{1,0:T(8,128)} async-done(((f32[64,2048]{1,0:T(8,128)}), f32[64,2048]{1,0:T(8,128)}) %all-reduce.6.cloned.1.call-update) | async-done | bytes 524304 | tf_op jit(solution)/shard_map/psum | solution.py:117
  728.8 0.3 fusion.3
  729.1 0.3 copy.34
  729.6 0.5 copy-done.2
  730.1 0.3 copy.45
  730.5 0.2 reshape.110
  730.9 0.3 broadcast_in_dim.68
  731.2 1.2 fusion.14
  732.4 72.1 %all-reduce.8.cloned.1.call-done = f32[64,2048]{1,0:T(8,128)} async-done(((f32[64,2048]{1,0:T(8,128)}), f32[64,2048]{1,0:T(8,128)}) %all-reduce.8.cloned.1.call-update) | async-done | bytes 524304 | tf_op jit(solution)/shard_map/psum | solution.py:118
  804.5 0.2 broadcast_in_dim.76
  804.7 0.2 broadcast_in_dim.75
  804.9 0.2 broadcast_in_dim.74
  805.1 2.2 fusion.16
  (47 shorter events, 1.8 us)
Async XLA Ops:
  7.2 4.4 copy-start.1
  7.2 5.3 copy-start
  7.2 5.3 copy-start.3
  7.2 57.1 %all-gather.4.cloned.1.call-start = ((), (), s32[]{:S(2)}) async-start(), calls=%async_computation | async-start | bytes 4325376 | tf_op jit(solution)/shard_map/all_gather | solution.py:86
  7.9 109.5 %all-gather.6.cloned.1.call-start = ((), (), s32[]{:S(2)}) async-start(), calls=%async_computation.1 | async-start | bytes 4325376 | tf_op jit(solution)/shard_map/all_gather | solution.py:87
  8.7 364.9 %all-reduce.4.cloned.1.call-start = ((), (), s32[]{:S(2)}) async-start(), calls=%async_computation.2 | async-start | bytes 524288 | tf_op jit(solution)/shard_map/psum | solution.py:14
  67.6 54.5 %copy-start.4 = (s32[256]{0:T(256)S(1)}, s32[256]{0:T(256)}, u32[]{:S(2)}) copy-start(s32[256]{0:T(256)} %param.13) | copy-start | bytes 3076
  121.4 330.7 %all-gather.8.cloned.1.call-start = ((), (), s32[]{:S(2)}) async-start(), calls=%async_computation.3 | async-start | bytes 17301504 | tf_op jit(solution)/shard_map/all_gather | solution.py:85
  122.0 606.8 %all-reduce.6.cloned.1.call-start = ((), (), s32[]{:S(2)}) async-start(), calls=%async_computation.4 | async-start | bytes 1048576 | tf_op jit(solution)/shard_map/psum | solution.py:117
  616.3 188.2 %all-reduce.8.cloned.1.call-start = ((), (), s32[]{:S(2)}) async-start(), calls=%async_computation.5 | async-start | bytes 1048576 | tf_op jit(solution)/shard_map/psum | solution.py:118
  729.1 1.0 copy-start.2
Sparse Core Ops, SparseCore 0:
  10.6 53.7 all-gather.3
  66.9 50.5 all-gather.5
  123.5 250.0 all-reduce.3
  376.0 76.1 all-gather.7
  616.4 112.3 all-reduce.5
  731.0 73.4 all-reduce.7
